TPU v7x, 32 devices: a whole 2x2x4 slice. The times are simulated.
32 devices in a mesh: dp: 8 (over z, y), tensor: 4 (over x, core).
Axes of the slice: x: 2, y: 2, z: 4, core: 2. Of those that a mesh axis runs over, the one named last changes fastest.
Arguments:
- signal: bfloat16 [26112, 512], P('dp', 'tensor'), may hold values from -6 to 6
- horizon: int32 [32], P('dp'), may hold values from 96 to 720, as said below
- down_a: bfloat16 [6144, 512], P('dp', 'tensor'), may hold values from -0.078125 to 0.078125
- iso_a: bfloat16 [34816, 512], P('dp', 'tensor'), may hold values from -0.046875 to 0.046875
- up_a: bfloat16 [512, 12, 512], P('dp', None, 'tensor'), may hold values from -0.25 to 0.25
- down_b: bfloat16 [8192, 512], P('dp', 'tensor'), may hold values from -0.0625 to 0.0625
- iso_b: bfloat16 [26112, 512], P('dp', 'tensor'), may hold values from -0.0546875 to 0.0546875
- up_b: bfloat16 [512, 16, 512], P('dp', None, 'tensor'), may hold values from -0.25 to 0.25
- merge_w: bfloat16 [1024, 512], P('dp', 'tensor'), may hold values from -0.1875 to 0.1875
- ff_in: bfloat16 [512, 2048], P(None, 'tensor'), may hold values from -0.25 to 0.25
- ff_out: bfloat16 [2048, 512], P('tensor'), may hold values from -0.125 to 0.125
- norm_gain: float32 [512], P('tensor'), may hold values from 0.1 to 1.9
- norm_bias: float32 [512], P('tensor'), may hold values from -4 to 4
- first_gain: float32 [512], P('tensor'), may hold values from 0.1 to 1.9
- first_bias: float32 [512], P('tensor'), may hold values from -4 to 4
- last_gain: float32 [512], P('tensor'), may hold values from 0.1 to 1.9
- last_bias: float32 [512], P('tensor'), may hold values from -4 to 4
- cotangent: bfloat16 [26112, 512], P('dp', 'tensor'), may hold values from -6 to 6
Outputs:
- series_out: bfloat16 [26112, 512], P('dp', 'tensor')
- grad_input: float32 [26112, 512], P('dp', 'tensor')
- grad_down_a: float32 [6144, 512], P('dp', 'tensor')
- grad_iso_a: float32 [34816, 512], P('dp', 'tensor')
- grad_up_a: float32 [512, 12, 512], P('dp', None, 'tensor')
- grad_down_b: float32 [8192, 512], P('dp', 'tensor')
- grad_iso_b: float32 [26112, 512], P('dp', 'tensor')
- grad_up_b: float32 [512, 16, 512], P('dp', None, 'tensor')
- grad_merge: float32 [1024, 512], P('dp', 'tensor')
- grad_ff_in: float32 [512, 2048], P(None, 'tensor')
- grad_ff_out: float32 [2048, 512], P('tensor')
- grad_norm_gain: float32 [512], P('tensor')
- grad_norm_bias: float32 [512], P('tensor')
- grad_first_gain: float32 [512], P('tensor')
- grad_first_bias: float32 [512], P('tensor')
- grad_last_gain: float32 [512], P('tensor')
- grad_last_bias: float32 [512], P('tensor')
Inputs may be any that keep to these rules, and one draw needn't show every extreme that they name: Each series' horizon is one of 96, 192, 336 and 720; some series has 720.
All inputs are finite; a program needn't handle non-finite values.
Results may differ from a plain program's by a relative error of at most 0.014.
Values may be sent and summed in bfloat16 or wider, within the bound.
No kernel may reach another device: no remote copies, remote signals or barrier semaphores. Data moves between devices by JAX's collectives and lax.ppermute only.
A program may use at most 384 MiB of HBM per device.

v0:
```python
from functools import partial
import jax
import jax.numpy as jnp
from jax import lax
from jax.sharding import PartitionSpec as P

D = 512
SA = 12
SB = 16
IN_LEN = 96
L = 816
MA = 68
MB = 51
EPS = 1e-05


def channel_gather(operand):
    return lax.all_gather(operand, "tensor", axis=1, tiled=True)


def channel_sum(operand):
    return lax.psum_scatter(operand, "tensor", scatter_dimension=1, tiled=True)


def row_totals(first, second):
    return lax.psum((first, second), "tensor")


def matmul(left, right):
    return jnp.dot(left, right, preferred_element_type=jnp.float32)


def over_rows(left, right):
    return lax.dot_general(
        left, right, (((0,), (0,)), ((), ())), preferred_element_type=jnp.float32
    )


def against(left, right):
    return lax.dot_general(
        left, right, (((1,), (1,)), ((), ())), preferred_element_type=jnp.float32
    )


def norm_forward(operand, gain_vec, bias_vec):
    row_total, row_square = row_totals(
        jnp.sum(operand, axis=1, keepdims=True), jnp.sum(operand * operand, axis=1, keepdims=True)
    )
    row_mean = row_total / D
    inv_std = lax.rsqrt(row_square / D - row_mean * row_mean + EPS)
    normed = (operand - row_mean) * inv_std
    return (normed * gain_vec + bias_vec, (normed, inv_std))


def norm_backward(upstream, gain_vec, stored):
    normed, inv_std = stored
    scaled = upstream * gain_vec
    first_sum, second_sum = row_totals(
        jnp.sum(scaled, axis=1, keepdims=True), jnp.sum(scaled * normed, axis=1, keepdims=True)
    )
    result = inv_std * (scaled - first_sum / D - normed * second_sum / D)
    return (result, jnp.sum(upstream * normed, axis=0), jnp.sum(upstream, axis=0))


def unfold(sequence, span_len):
    padded = jnp.pad(sequence, ((0, 0), (span_len - 1, 0), (0, 0)))
    return jnp.concatenate(
        [padded[:, offset : offset + span_len, :] for offset in range(span_len)], axis=2
    )


def fold(windows, series_count, span_len):
    zeros_in = jnp.zeros((series_count, span_len, D), jnp.float32)
    _, back = jax.vjp(lambda seq_in: unfold(seq_in, span_len), zeros_in)
    return back(windows)[0]


def body(
    signal,
    horizon,
    down_a,
    iso_a,
    up_a,
    down_b,
    iso_b,
    up_b,
    merge_w,
    ff_in,
    ff_out,
    norm_gain,
    norm_bias,
    first_gain,
    first_bias,
    last_gain,
    last_bias,
    cotangent,
):
    row_count = signal.shape[0]
    col_count = signal.shape[1]
    series_count = row_count // L
    short_a = row_count // SA
    short_b = row_count // SB
    wd_a, wi_a, wu_a, wd_b, wi_b, wu_b, w_merge = (
        lax.all_gather(down_a, "dp", axis=0, tiled=True),
        lax.all_gather(iso_a, "dp", axis=0, tiled=True),
        lax.all_gather(up_a, "dp", axis=0, tiled=True),
        lax.all_gather(down_b, "dp", axis=0, tiled=True),
        lax.all_gather(iso_b, "dp", axis=0, tiled=True),
        lax.all_gather(up_b, "dp", axis=0, tiled=True),
        lax.all_gather(merge_w, "dp", axis=0, tiled=True),
    )
    x_full = channel_gather(signal)
    x_float = signal.astype(jnp.float32)
    window_a = x_full.reshape(short_a, SA * D)
    window_b = x_full.reshape(short_b, SB * D)
    down_act_a = jnp.tanh(matmul(window_a, wd_a))
    down_act_b = jnp.tanh(matmul(window_b, wd_b))
    down_low_a = down_act_a.astype(jnp.bfloat16)
    down_low_b = down_act_b.astype(jnp.bfloat16)
    down_full = channel_gather(jnp.concatenate([down_low_a, down_low_b], axis=0))
    taps_a = unfold(down_full[:short_a].reshape(series_count, MA, D), MA).reshape(short_a, MA * D)
    taps_b = unfold(down_full[short_a:].reshape(series_count, MB, D), MB).reshape(short_b, MB * D)
    iso_act_a = jnp.tanh(matmul(taps_a, wi_a))
    iso_act_b = jnp.tanh(matmul(taps_b, wi_b))
    middle_a, store_mid_a = norm_forward(
        iso_act_a + down_low_a.astype(jnp.float32), norm_gain, norm_bias
    )
    middle_b, store_mid_b = norm_forward(
        iso_act_b + down_low_b.astype(jnp.float32), norm_gain, norm_bias
    )
    middle_full = channel_gather(jnp.concatenate([middle_a, middle_b], axis=0).astype(jnp.bfloat16))
    mid_full_a = middle_full[:short_a]
    mid_full_b = middle_full[short_a:]
    up_act_a = jnp.tanh(
        matmul(mid_full_a, wu_a.reshape(D, SA * col_count)).reshape(row_count, col_count)
    )
    up_act_b = jnp.tanh(
        matmul(mid_full_b, wu_b.reshape(D, SB * col_count)).reshape(row_count, col_count)
    )
    branch_a, store_br_a = norm_forward(up_act_a + x_float, norm_gain, norm_bias)
    branch_b, store_br_b = norm_forward(up_act_b + x_float, norm_gain, norm_bias)
    pair_full = channel_gather(jnp.concatenate([branch_a, branch_b], axis=0).astype(jnp.bfloat16))
    merge_in = jnp.concatenate([pair_full[:row_count], pair_full[row_count:]], axis=1)
    merged = matmul(merge_in, w_merge)
    first_out, store_first = norm_forward(merged, first_gain, first_bias)
    first_full = channel_gather(first_out.astype(jnp.bfloat16))
    hidden_pre = matmul(first_full, ff_in)
    hidden = jax.nn.gelu(hidden_pre, approximate=False).astype(jnp.bfloat16)
    feed = channel_sum(matmul(hidden, ff_out))
    last_out, store_last = norm_forward(merged + feed, last_gain, last_bias)
    positions = lax.broadcasted_iota(jnp.int32, (series_count, L), 1)
    out_mask = (positions < IN_LEN + horizon[:, None]).astype(jnp.float32).reshape(row_count, 1)
    series_out = (last_out * out_mask).astype(jnp.bfloat16)
    upstream = cotangent.astype(jnp.float32) * out_mask
    grad_sum, grad_last_gain, grad_last_bias = norm_backward(upstream, last_gain, store_last)
    grad_feed = channel_gather(grad_sum.astype(jnp.bfloat16))
    grad_ff_out = over_rows(hidden, grad_feed)
    grad_hidden = against(grad_feed, ff_out)
    _, gelu_back = jax.vjp(partial(jax.nn.gelu, approximate=False), hidden_pre)
    grad_hpre = gelu_back(grad_hidden)[0].astype(jnp.bfloat16)
    grad_ff_in = over_rows(first_full, grad_hpre)
    grad_first = channel_sum(against(grad_hpre, ff_in))
    grad_merged_norm, grad_first_gain, grad_first_bias = norm_backward(
        grad_first, first_gain, store_first
    )
    grad_merged = (grad_merged_norm + grad_sum).astype(jnp.bfloat16)
    grad_merge = over_rows(merge_in, grad_merged)
    grad_pair_full = against(grad_merged, w_merge)
    grad_pair = channel_sum(jnp.concatenate([grad_pair_full[:, :D], grad_pair_full[:, D:]], axis=0))
    grad_resid_a, gain_part_one, bias_part_one = norm_backward(
        grad_pair[:row_count], norm_gain, store_br_a
    )
    grad_resid_b, gain_part_two, bias_part_two = norm_backward(
        grad_pair[row_count:], norm_gain, store_br_b
    )
    grad_upre_a = (
        (grad_resid_a * (1.0 - up_act_a * up_act_a))
        .astype(jnp.bfloat16)
        .reshape(short_a, SA * col_count)
    )
    grad_upre_b = (
        (grad_resid_b * (1.0 - up_act_b * up_act_b))
        .astype(jnp.bfloat16)
        .reshape(short_b, SB * col_count)
    )
    grad_up_a = over_rows(mid_full_a, grad_upre_a).reshape(D, SA, col_count)
    grad_up_b = over_rows(mid_full_b, grad_upre_b).reshape(D, SB, col_count)
    grad_mid_full_a = against(grad_upre_a, wu_a.reshape(D, SA * col_count))
    grad_mid_full_b = against(grad_upre_b, wu_b.reshape(D, SB * col_count))
    grad_middle = channel_sum(jnp.concatenate([grad_mid_full_a, grad_mid_full_b], axis=0))
    grad_inner_a, gain_part_three, bias_part_three = norm_backward(
        grad_middle[:short_a], norm_gain, store_mid_a
    )
    grad_inner_b, gain_part_four, bias_part_four = norm_backward(
        grad_middle[short_a:], norm_gain, store_mid_b
    )
    grad_ipre_a = (grad_inner_a * (1.0 - iso_act_a * iso_act_a)).astype(jnp.bfloat16)
    grad_ipre_b = (grad_inner_b * (1.0 - iso_act_b * iso_act_b)).astype(jnp.bfloat16)
    grad_iso_a = over_rows(taps_a, grad_ipre_a)
    grad_iso_b = over_rows(taps_b, grad_ipre_b)
    grad_taps_a = fold(
        against(grad_ipre_a, wi_a).reshape(series_count, MA, MA * D), series_count, MA
    ).reshape(short_a, D)
    grad_taps_b = fold(
        against(grad_ipre_b, wi_b).reshape(series_count, MB, MB * D), series_count, MB
    ).reshape(short_b, D)
    grad_down = channel_sum(jnp.concatenate([grad_taps_a, grad_taps_b], axis=0))
    grad_dpre_a = ((grad_down[:short_a] + grad_inner_a) * (1.0 - down_act_a * down_act_a)).astype(
        jnp.bfloat16
    )
    grad_dpre_b = ((grad_down[short_a:] + grad_inner_b) * (1.0 - down_act_b * down_act_b)).astype(
        jnp.bfloat16
    )
    grad_down_a = over_rows(window_a, grad_dpre_a)
    grad_down_b = over_rows(window_b, grad_dpre_b)
    grad_x_full = against(grad_dpre_a, wd_a).reshape(row_count, D) + against(
        grad_dpre_b, wd_b
    ).reshape(row_count, D)
    grad_input = channel_sum(grad_x_full) + grad_resid_a + grad_resid_b
    sum_down_a, sum_iso_a, sum_up_a, sum_down_b, sum_iso_b, sum_up_b, sum_merge = (
        lax.psum_scatter(grad_down_a, "dp", scatter_dimension=0, tiled=True),
        lax.psum_scatter(grad_iso_a, "dp", scatter_dimension=0, tiled=True),
        lax.psum_scatter(grad_up_a, "dp", scatter_dimension=0, tiled=True),
        lax.psum_scatter(grad_down_b, "dp", scatter_dimension=0, tiled=True),
        lax.psum_scatter(grad_iso_b, "dp", scatter_dimension=0, tiled=True),
        lax.psum_scatter(grad_up_b, "dp", scatter_dimension=0, tiled=True),
        lax.psum_scatter(grad_merge, "dp", scatter_dimension=0, tiled=True),
    )
    grad_norm_gain = gain_part_one + gain_part_two + gain_part_three + gain_part_four
    grad_norm_bias = bias_part_one + bias_part_two + bias_part_three + bias_part_four
    (
        sum_ff_in,
        sum_ff_out,
        sum_norm_gain,
        sum_norm_bias,
        sum_first_gain,
        sum_first_bias,
        sum_last_gain,
        sum_last_bias,
    ) = lax.psum(
        (
            grad_ff_in,
            grad_ff_out,
            grad_norm_gain,
            grad_norm_bias,
            grad_first_gain,
            grad_first_bias,
            grad_last_gain,
            grad_last_bias,
        ),
        "dp",
    )
    return (
        series_out,
        grad_input,
        sum_down_a,
        sum_iso_a,
        sum_up_a,
        sum_down_b,
        sum_iso_b,
        sum_up_b,
        sum_merge,
        sum_ff_in,
        sum_ff_out,
        sum_norm_gain,
        sum_norm_bias,
        sum_first_gain,
        sum_first_bias,
        sum_last_gain,
        sum_last_bias,
    )


def solution(mesh):
    in_specs = (
        P("dp", "tensor"),
        P("dp"),
        P("dp", "tensor"),
        P("dp", "tensor"),
        P("dp", None, "tensor"),
        P("dp", "tensor"),
        P("dp", "tensor"),
        P("dp", None, "tensor"),
        P("dp", "tensor"),
        P(None, "tensor"),
        P("tensor", None),
        P("tensor"),
        P("tensor"),
        P("tensor"),
        P("tensor"),
        P("tensor"),
        P("tensor"),
        P("dp", "tensor"),
    )
    out_specs = (
        P("dp", "tensor"),
        P("dp", "tensor"),
        P("dp", "tensor"),
        P("dp", "tensor"),
        P("dp", None, "tensor"),
        P("dp", "tensor"),
        P("dp", "tensor"),
        P("dp", None, "tensor"),
        P("dp", "tensor"),
        P(None, "tensor"),
        P("tensor", None),
        P("tensor"),
        P("tensor"),
        P("tensor"),
        P("tensor"),
        P("tensor"),
        P("tensor"),
    )
    return jax.shard_map(body, mesh=mesh, in_specs=in_specs, out_specs=out_specs, check_vma=False)
```

profile of v0, /device:TPU:0, one launch (start us, length us, event | category | flops | bytes accessed | tf_op | source)
XLA Modules:
  0.0 2445.4 jit_solution(7700934560776956939)
XLA Ops:
  12.0 45.2 %all-gather.21.cloned.1.call-done = bf16[512,12,128]{2,0,1:T(8,128)(2,1)} async-done(((bf16[64,12,128]{2,0,1:T(8,128)(2,1)}), bf16[512,12,128]{2,0,1:T(8,128)(2,1)}) %all-gather.21.cloned.1.call-update) | async-done | bytes 1572880 | tf_op jit(solution)/shard_map/all_gather | solution.py:106
  59.7 27.9 %all-gather.11.cloned.1.call-done = bf16[3264,512]{1,0:T(8,128)(2,1)} async-done(((bf16[3264,128]{1,0:T(8,128)(2,1)}), bf16[3264,512]{1,0:T(8,128)(2,1)}) %all-gather.11.cloned.1.call-update) | async-done | bytes 3342352 | tf_op jit(solution)/shard_map/all_gather | solution.py:18
  101.1 38.0 %all-gather.15.cloned.1.call-done = bf16[8192,128]{1,0:T(8,128)(2,1)} async-done(((bf16[1024,128]{1,0:T(8,128)(2,1)}), bf16[8192,128]{1,0:T(8,128)(2,1)}) %all-gather.15.cloned.1.call-update) | async-done | bytes 2097168 | tf_op jit(solution)/shard_map/all_gather | solution.py:107
  143.4 40.4 %all-gather.13.cloned.1.call-done = bf16[6144,128]{1,0:T(8,128)(2,1)} async-done(((bf16[768,128]{1,0:T(8,128)(2,1)}), bf16[6144,128]{1,0:T(8,128)(2,1)}) %all-gather.13.cloned.1.call-update) | async-done | bytes 1572880 | tf_op jit(solution)/shard_map/all_gather | solution.py:104
  525.9 14.1 fusion.39
  567.0 12.4 all-reduce.129
  586.2 32.9 %all_gather.49 = bf16[1024,128]{1,0:T(8,128)(2,1)} all-gather(bf16[128,128]{1,0:T(8,128)(2,1)S(1)} %copy-done.172), channel_id=1, replica_groups=mesh['dp'=8,'tensor'=4] {'dp'}, dimensions={0}, use_global_device_ids=true | all-gather | bytes 294912 | tf_op jit(solution)/shard_map/all_gather | solution.py:110
  619.1 15.2 all-gather.25.cloned.1.call-done
  655.5 31.2 %all-gather.27.cloned.1.call-done = bf16[3264,512]{1,0:T(8,128)(2,1)} async-done(((bf16[3264,128]{1,0:T(8,128)(2,1)}), bf16[3264,512]{1,0:T(8,128)(2,1)}) %all-gather.27.cloned.1.call-update) | async-done | bytes 3342352 | tf_op jit(solution)/shard_map/all_gather | solution.py:18
  686.7 18.5 multiply_convert_fusion
  712.0 60.9 %reduce-scatter.14.cloned.1.call-done = f32[3264,128]{1,0:T(8,128)} async-done(((f32[3264,512]{1,0:T(8,128)}), f32[3264,128]{1,0:T(8,128)}) %reduce-scatter.14.cloned.1.call-update) | async-done | bytes 1671184 | tf_op jit(solution)/shard_map/reduce_scatter | solution.py:22
  814.4 31.4 %all-gather.29.cloned.1.call-done = bf16[3264,512]{1,0:T(8,128)(2,1)} async-done(((bf16[3264,128]{1,0:T(8,128)(2,1)}), bf16[3264,512]{1,0:T(8,128)(2,1)}) %all-gather.29.cloned.1.call-update) | async-done | bytes 3342352 | tf_op jit(solution)/shard_map/all_gather | solution.py:18
  862.2 61.1 %reduce-scatter.16.cloned.1.call-done = f32[3264,128]{1,0:T(8,128)} async-done(((f32[3264,512]{1,0:T(8,128)}), f32[3264,128]{1,0:T(8,128)}) %reduce-scatter.16.cloned.1.call-update) | async-done | bytes 1671184 | tf_op jit(solution)/shard_map/reduce_scatter | solution.py:22
  977.6 105.6 %reduce-scatter.18.cloned.1.call-done = f32[6528,128]{1,0:T(8,128)} async-done(((f32[6528,512]{1,0:T(8,128)}), f32[6528,128]{1,0:T(8,128)}) %reduce-scatter.18.cloned.1.call-update) | async-done | bytes 3342352 | tf_op jit(solution)/shard_map/reduce_scatter | solution.py:22
  1117.3 25.8 %reduce-scatter.20.cloned.1.call-done = f32[476,128]{1,0:T(8,128)} async-done(((f32[476,512]{1,0:T(8,128)}), f32[476,128]{1,0:T(8,128)}) %reduce-scatter.20.cloned.1.call-update) | async-done | bytes 243728 | tf_op jit(solution)/shard_map/reduce_scatter | solution.py:22
  1152.7 13.2 fusion.58
  1165.9 17.5 reshape.245
  1202.4 17.3 fusion.60
  1219.7 30.3 %reshape.243 = f32[4,68,34816]{2,1,0:T(8,128)} reshape(f32[272,34816]{1,0:T(8,128)} %fusion.60) | data formatting | bytes 75759616 | tf_op jit(solution)/shard_map/reshape | solution.py:202
  1289.8 14.3 pad_add_fusion
  1311.6 22.4 reduce-scatter.22.cloned.1.call-done
  1397.5 12.8 fusion.57
  1410.4 15.0 fusion.59
  1426.2 22.4 all-reduce.121
  1450.8 53.4 %reduce-scatter.26.cloned.1.call-done = f32[768,128]{0,1:T(8,128)} async-done(((f32[6144,128]{0,1:T(8,128)}), f32[768,128]{0,1:T(8,128)}) %reduce-scatter.26.cloned.1.call-update) | async-done | bytes 393232 | tf_op jit(solution)/shard_map/reduce_scatter | solution.py:221
  1506.0 89.6 %reduce-scatter.32.cloned.1.call-done = f32[1024,128]{0,1:T(8,128)} async-done(((f32[8192,128]{0,1:T(8,128)}), f32[1024,128]{0,1:T(8,128)}) %reduce-scatter.32.cloned.1.call-update) | async-done | bytes 524304 | tf_op jit(solution)/shard_map/reduce_scatter | solution.py:224
  1597.7 61.2 %reduce-scatter.24.cloned.1.call-done = f32[3264,128]{1,0:T(8,128)} async-done(((f32[3264,512]{1,0:T(8,128)}), f32[3264,128]{1,0:T(8,128)}) %reduce-scatter.24.cloned.1.call-update) | async-done | bytes 1671184 | tf_op jit(solution)/shard_map/reduce_scatter | solution.py:22
  1667.6 98.2 %all-reduce.133.cloned.1.call-done = (f32[512,512]{1,0:T(8,128)}, f32[512,512]{1,0:T(8,128)}) async-done(((f32[512,512]{1,0:T(8,128)}, f32[512,512]{1,0:T(8,128)}), (f32[512,512]{1,0:T(8,128)}, f32[512,512]{1,0:T(8,128)})) %all-reduce.133.cloned.1.call-update) | async-done | bytes 2097168 | tf_op jit(solution)/shard_map/psum | solution.py:240
  1765.8 66.0 %reduce-scatter.38.cloned.1.call-done = f32[128,128]{1,0:T(8,128)} async-done(((f32[1024,128]{1,0:T(8,128)}), f32[128,128]{1,0:T(8,128)}) %reduce-scatter.38.cloned.1.call-update) | async-done | bytes 65552 | tf_op jit(solution)/shard_map/reduce_scatter | solution.py:227
  1831.8 78.1 %reduce-scatter.30.cloned.1.call-done = f32[64,12,128]{2,0,1:T(8,128)} async-done(((f32[512,12,128]{2,0,1:T(8,128)}), f32[64,12,128]{2,0,1:T(8,128)}) %reduce-scatter.30.cloned.1.call-update) | async-done | bytes 393232 | tf_op jit(solution)/shard_map/reduce_scatter | solution.py:223
  1909.9 221.7 %reduce-scatter.34.cloned.1.call-done = f32[3264,128]{1,0:T(8,128)} async-done(((f32[26112,128]{1,0:T(8,128)}), f32[3264,128]{1,0:T(8,128)}) %reduce-scatter.34.cloned.1.call-update) | async-done | bytes 1671184 | tf_op jit(solution)/shard_map/reduce_scatter | solution.py:225
  2131.6 302.3 %reduce-scatter.28.cloned.1.call-done = f32[4352,128]{1,0:T(8,128)} async-done(((f32[34816,128]{1,0:T(8,128)}), f32[4352,128]{1,0:T(8,128)}) %reduce-scatter.28.cloned.1.call-update) | async-done | bytes 2228240 | tf_op jit(solution)/shard_map/reduce_scatter | solution.py:222
  (798 shorter events, 732.7 us)
Async XLA Ops:
  7.2 679.5 %copy-start = (bf16[512,512]{1,0:T(8,128)(2,1)S(1)}, bf16[512,512]{1,0:T(8,128)(2,1)}, u32[]{:S(2)}) copy-start(bf16[512,512]{1,0:T(8,128)(2,1)} %param.27) | copy-start | bytes 1572868
  7.2 49.9 %all-gather.21.cloned.1.call-start = ((), (), s32[]{:S(2)}) async-start(), calls=%async_computation.18 | async-start | bytes 1769472 | tf_op jit(solution)/shard_map/all_gather | solution.py:106
  7.9 79.7 %all-gather.11.cloned.1.call-start = ((), (), s32[]{:S(2)}) async-start(), calls=%async_computation.13 | async-start | bytes 4177920 | tf_op jit(solution)/shard_map/all_gather | solution.py:18
  8.7 130.4 %all-gather.15.cloned.1.call-start = ((), (), s32[]{:S(2)}) async-start(), calls=%async_computation.15 | async-start | bytes 2359296 | tf_op jit(solution)/shard_map/all_gather | solution.py:107
  9.4 174.4 %all-gather.13.cloned.1.call-start = ((), (), s32[]{:S(2)}) async-start(), calls=%async_computation.14 | async-start | bytes 1769472 | tf_op jit(solution)/shard_map/all_gather | solution.py:104
  10.0 506.6 %all-gather.19.cloned.1.call-start = ((), (), s32[]{:S(2)}) async-start(), calls=%async_computation.17 | async-start | bytes 7520256 | tf_op jit(solution)/shard_map/all_gather | solution.py:108
  10.6 515.3 %all-gather.17.cloned.1.call-start = ((), (), s32[]{:S(2)}) async-start(), calls=%async_computation.16 | async-start | bytes 10027008 | tf_op jit(solution)/shard_map/all_gather | solution.py:105
  11.2 546.7 %all-gather.23.cloned.1.call-start = ((), (), s32[]{:S(2)}) async-start(), calls=%async_computation.19 | async-start | bytes 2359296 | tf_op jit(solution)/shard_map/all_gather | solution.py:109
  11.9 622.4 %all-gather.25.cloned.1.call-start = ((), (), s32[]{:S(2)}) async-start(), calls=%async_computation.20 | async-start | bytes 8355840 | tf_op jit(solution)/shard_map/all_gather | solution.py:18
  563.0 537.5 %copy-start.2 = (f32[3264,128]{1,0:T(8,128)}, f32[3264,128]{1,0:T(8,128)S(1)}, u32[]{:S(2)}) copy-start(f32[3264,128]{1,0:T(8,128)S(1)} %tanh.31) | copy-start | bytes 5013508
  580.3 520.2 %copy-start.147 = (f32[3264]{0:T(1024)}, f32[3264]{0:T(1024)S(1)}, u32[]{:S(2)}) copy-start(f32[3264]{0:T(1024)S(1)} %get-tuple-element.114) | copy-start | bytes 39172
  580.4 520.2 %copy-start.149 = (f32[3264]{0:T(1024)}, f32[3264]{0:T(1024)S(1)}, u32[]{:S(2)}) copy-start(f32[3264]{0:T(1024)S(1)} %get-tuple-element.115) | copy-start | bytes 39172
  580.4 520.2 %copy-start.151 = (f32[3264]{0:T(1024)}, f32[3264]{0:T(1024)S(1)}, u32[]{:S(2)}) copy-start(f32[3264]{0:T(1024)S(1)} %get-tuple-element.409) | copy-start | bytes 39172
  580.4 520.2 %copy-start.153 = (f32[3264]{0:T(1024)}, f32[3264]{0:T(1024)S(1)}, u32[]{:S(2)}) copy-start(f32[3264]{0:T(1024)S(1)} %get-tuple-element.410) | copy-start | bytes 39172
  586.2 100.5 %all-gather.27.cloned.1.call-start = ((), (), s32[]{:S(2)}) async-start(), calls=%async_computation.21 | async-start | bytes 4177920 | tf_op jit(solution)/shard_map/all_gather | solution.py:18
  655.4 117.5 %reduce-scatter.14.cloned.1.call-start = ((), (), s32[]{:S(2)}) async-start(), calls=%async_computation.22 | async-start | bytes 8355840 | tf_op jit(solution)/shard_map/reduce_scatter | solution.py:22
  711.7 134.0 %all-gather.29.cloned.1.call-start = ((), (), s32[]{:S(2)}) async-start(), calls=%async_computation.23 | async-start | bytes 4177920 | tf_op jit(solution)/shard_map/all_gather | solution.py:18
  814.3 108.9 %reduce-scatter.16.cloned.1.call-start = ((), (), s32[]{:S(2)}) async-start(), calls=%async_computation.24 | async-start | bytes 8355840 | tf_op jit(solution)/shard_map/reduce_scatter | solution.py:22
  862.1 221.1 %reduce-scatter.18.cloned.1.call-start = ((), (), s32[]{:S(2)}) async-start(), calls=%async_computation.25 | async-start | bytes 16711680 | tf_op jit(solution)/shard_map/reduce_scatter | solution.py:22
  977.6 165.6 %reduce-scatter.20.cloned.1.call-start = ((), (), s32[]{:S(2)}) async-start(), calls=%async_computation.26 | async-start | bytes 1228800 | tf_op jit(solution)/shard_map/reduce_scatter | solution.py:22
  1117.3 216.8 %reduce-scatter.22.cloned.1.call-start = ((), (), s32[]{:S(2)}) async-start(), calls=%async_computation.27 | async-start | bytes 1228800 | tf_op jit(solution)/shard_map/reduce_scatter | solution.py:22
  1308.3 140.3 %reduce-scatter.36.cloned.1.call-start = ((), (), s32[]{:S(2)}) async-start(), calls=%async_computation.34 | async-start | bytes 4718592 | tf_op jit(solution)/shard_map/reduce_scatter | solution.py:226
  1311.4 192.7 %reduce-scatter.26.cloned.1.call-start = ((), (), s32[]{:S(2)}) async-start(), calls=%async_computation.29 | async-start | bytes 3538944 | tf_op jit(solution)/shard_map/reduce_scatter | solution.py:221
  1339.8 255.8 %reduce-scatter.32.cloned.1.call-start = ((), (), s32[]{:S(2)}) async-start(), calls=%async_computation.32 | async-start | bytes 4718592 | tf_op jit(solution)/shard_map/reduce_scatter | solution.py:224
  1345.9 313.0 %reduce-scatter.24.cloned.1.call-start = ((), (), s32[]{:S(2)}) async-start(), calls=%async_computation.28 | async-start | bytes 8355840 | tf_op jit(solution)/shard_map/reduce_scatter | solution.py:22
  1379.3 386.5 %all-reduce.133.cloned.1.call-start = ((), (), s32[]{:S(2)}) async-start(), calls=%async_computation.36 | async-start | bytes 4194304 | tf_op jit(solution)/shard_map/psum | solution.py:240
  1388.5 443.3 %reduce-scatter.38.cloned.1.call-start = ((), (), s32[]{:S(2)}) async-start(), calls=%async_computation.35 | async-start | bytes 589824 | tf_op jit(solution)/shard_map/reduce_scatter | solution.py:227
  1394.5 515.4 %reduce-scatter.30.cloned.1.call-start = ((), (), s32[]{:S(2)}) async-start(), calls=%async_computation.31 | async-start | bytes 3538944 | tf_op jit(solution)/shard_map/reduce_scatter | solution.py:223
  1397.3 734.3 %reduce-scatter.34.cloned.1.call-start = ((), (), s32[]{:S(2)}) async-start(), calls=%async_computation.33 | async-start | bytes 15040512 | tf_op jit(solution)/shard_map/reduce_scatter | solution.py:225
  1410.4 1023.5 %reduce-scatter.28.cloned.1.call-start = ((), (), s32[]{:S(2)}) async-start(), calls=%async_computation.30 | async-start | bytes 20054016 | tf_op jit(solution)/shard_map/reduce_scatter | solution.py:222
  1425.5 233.4 %copy-start.3 = (f32[3264,128]{1,0:T(8,128)S(1)}, f32[3264,128]{1,0:T(8,128)}, u32[]{:S(2)}) copy-start(f32[3264,128]{1,0:T(8,128)} %copy-done.2) | copy-start | bytes 5013508
  1595.6 842.7 %copy-start.1 = (bf16[512,512]{1,0:T(8,128)(2,1)S(1)}, bf16[512,512]{1,0:T(8,128)(2,1)}, u32[]{:S(2)}) copy-start(bf16[512,512]{1,0:T(8,128)(2,1)} %param.27) | copy-start | bytes 1572868
  (184 other events, 5703.2 us)
Sparse Core Ops, SparseCore 0:
  10.2 46.8 all-gather.20
  58.7 28.8 all-gather.10
  89.7 49.2 all-gather.14
  141.1 42.6 all-gather.12
  185.8 102.7 all-gather.18
  290.6 129.7 all-gather.16
  422.6 47.4 all-gather.22
  586.3 47.9 all-gather.24
  655.5 31.1 all-gather.26
  711.9 60.9 reduce-scatter.13
  814.5 31.2 all-gather.28
  862.2 60.9 reduce-scatter.15
  977.7 105.4 reduce-scatter.17
  1117.4 25.7 reduce-scatter.19
  1308.4 25.6 reduce-scatter.21
  1337.5 88.2 reduce-scatter.35
  1429.7 74.3 reduce-scatter.25
  1508.0 87.5 reduce-scatter.31
  1598.2 60.7 reduce-scatter.23
  1663.5 102.2 all-reduce.132
  1770.1 61.6 reduce-scatter.37
  1836.0 73.8 reduce-scatter.29
  1914.1 217.3 reduce-scatter.33
  2136.4 297.3 reduce-scatter.27
where the time goes:
time: 2460 us; the launch traced here: 2450 us
  waiting for transfers between devices  1480 us (60%)
  local copies, waits for them, and re-layouts  493 us (20%)
  matrix products  186 us (8%)
  blocking collectives  149 us (6%)
  other arithmetic  120 us (5%)
    reduce_scatter x6, waiting for transfers between devices, channel_sum(): return lax.psum_scatter(operand, 'tensor', scatter_dimension=1, tiled=True)  337 us
    reduce_scatter x1, waiting for transfers between devices, body(): lax.psum_scatter(grad_iso_a, 'dp', scatter_dimension=0, tiled=True)  302 us
    reduce_scatter x1, waiting for transfers between devices, body(): lax.psum_scatter(grad_iso_b, 'dp', scatter_dimension=0, tiled=True)  222 us
    concatenate x119, local copies, waits for them, and re-layouts, unfold(): jnp.concatenate([padded[:, offset:offset + span_len, :] for offset in ran...  191 us
    unnamed x507, local copies, waits for them, and re-layouts  133 us
    all_gather x4, waiting for transfers between devices, channel_gather(): return lax.all_gather(operand, 'tensor', axis=1, tiled=True)  106 us
    psum x1, waiting for transfers between devices, body(): lax.psum((grad_ff_in, grad_ff_out, grad_norm_gain, grad_norm_bias, grad_f...  98.2 us
    reduce_scatter x1, waiting for transfers between devices, body(): lax.psum_scatter(grad_down_b, 'dp', scatter_dimension=0, tiled=True)  89.6 us
  transfers between devices with their start and end apart: 24, of which 20 were waited for; matrix products, arithmetic and copies ran while one was open for 20% of the time, Pallas kernels for 0%

commit v1 on v0

--- a/solution.py
+++ b/solution.py
@@ -14,8 +14,24 @@
 EPS = 1e-05
 
 
+def ring_gather(x, axis, dim):
+    ways, here, turn = (lax.axis_size(axis), lax.axis_index(axis), x.shape[dim])
+    lengths = [n * ways if d == dim else n for d, n in enumerate(x.shape)]
+    full = lax.dynamic_update_slice_in_dim(jnp.zeros(lengths, x.dtype), x, here * turn, axis=dim)
+    going_up = going_down = x
+    for far in range(1, ways // 2 + 1):
+        going_up = lax.ppermute(going_up, axis, [(d, (d + 1) % ways) for d in range(ways)])
+        full = lax.dynamic_update_slice_in_dim(full, going_up, (here - far) % ways * turn, axis=dim)
+        if 2 * far < ways:
+            going_down = lax.ppermute(going_down, axis, [(d, (d - 1) % ways) for d in range(ways)])
+            full = lax.dynamic_update_slice_in_dim(
+                full, going_down, (here + far) % ways * turn, axis=dim
+            )
+    return full
+
+
 def channel_gather(operand):
-    return lax.all_gather(operand, "tensor", axis=1, tiled=True)
+    return ring_gather(operand, "tensor", 1)
 
 
 def channel_sum(operand):

time: 2460 us -> 2400 us (0.976)
  waiting for transfers between devices: 1480 us -> 1420 us
    ppermute x0 -> x18, waiting for transfers between devices: none -> 117 us  [the longest x12 117 us: ring_gather(): lax.ppermute(going_up, axis, [(d, (d + 1) % ways) for d in range(ways)])]
    all_gather x4 -> x0, waiting for transfers between devices: 106 us -> none  [channel_gather(): return lax.all_gather(operand, 'tensor', axis=1, tiled=True)]
    all_gather x1, waiting for transfers between devices: 45.2 us -> 0.01 us  [body(): lax.all_gather(up_a, 'dp', axis=0, tiled=True)]
    all_gather x1, waiting for transfers between devices: 40.4 us -> 1.45 us  [body(): lax.all_gather(down_a, 'dp', axis=0, tiled=True)]
    reduce_scatter x1, waiting for transfers between devices: 53.4 us -> 78.3 us  [body(): lax.psum_scatter(grad_down_a, 'dp', scatter_dimension=0, tiled=True)]
    unnamed x507 -> x513, local copies, waits for them, and re-layouts: 133 us -> 128 us
  transfers between devices with their start and end apart: 24 -> 38, of which waited for: 20 -> 27; matrix products, arithmetic and copies ran while one was open for 20% -> 20% of each run, Pallas kernels for 0% -> 0%
where the time goes in v1:
time: 2400 us; the launch traced here: 2390 us
  waiting for transfers between devices  1420 us (59%)
  local copies, waits for them, and re-layouts  496 us (21%)
  matrix products  183 us (8%)
  blocking collectives  131 us (5%)
  other arithmetic  117 us (5%)
    reduce_scatter x6, waiting for transfers between devices, channel_sum(): return lax.psum_scatter(operand, 'tensor', scatter_dimension=1, tiled=True)  319 us
    reduce_scatter x1, waiting for transfers between devices, body(): lax.psum_scatter(grad_iso_a, 'dp', scatter_dimension=0, tiled=True)  302 us
    reduce_scatter x1, waiting for transfers between devices, body(): lax.psum_scatter(grad_iso_b, 'dp', scatter_dimension=0, tiled=True)  222 us
    concatenate x119, local copies, waits for them, and re-layouts, unfold(): jnp.concatenate([padded[:, offset:offset + span_len, :] for offset in ran...  191 us
    unnamed x513, local copies, waits for them, and re-layouts  128 us
    ppermute x12, waiting for transfers between devices, ring_gather(): lax.ppermute(going_up, axis, [(d, (d + 1) % ways) for d in range(ways)])  117 us
    psum x1, waiting for transfers between devices, body(): lax.psum((grad_ff_in, grad_ff_out, grad_norm_gain, grad_norm_bias, grad_f...  97.6 us
    reduce_scatter x1, waiting for transfers between devices, body(): lax.psum_scatter(grad_down_b, 'dp', scatter_dimension=0, tiled=True)  91.7 us
  transfers between devices with their start and end apart: 38, of which 27 were waited for; matrix products, arithmetic and copies ran while one was open for 20% of the time, Pallas kernels for 0%

profile of v1, /device:TPU:0, one launch (start us, length us, event | category | flops | bytes accessed | tf_op | source)
XLA Modules:
  0.0 2390.2 jit_solution(1575661926001045654)
XLA Ops:
  16.8 12.4 collective-permute-done
  61.3 46.1 %all-gather.9.cloned.1.call-done = bf16[8192,128]{1,0:T(8,128)(2,1)} async-done(((bf16[1024,128]{1,0:T(8,128)(2,1)}), bf16[8192,128]{1,0:T(8,128)(2,1)}) %all-gather.9.cloned.1.call-update) | async-done | bytes 2097168 | tf_op jit(solution)/shard_map/all_gather | solution.py:123
  451.3 14.1 fusion.39
  494.2 12.4 all-reduce.129
  514.7 34.4 %collective-permute-done.9 = bf16[6528,128]{1,0:T(8,128)(2,1)S(1)} collective-permute-done((bf16[6528,128]{1,0:T(8,128)(2,1)S(1)}, bf16[6528,128]{1,0:T(8,128)(2,1)S(1)}, u32[]{:S(2)}, u32[]{:S(2)}) %collective-permute-start.9) | collective-permute-done | bytes 1671200 | tf_op jit(solution)/shard_map/ppermute | solution.py:23
  551.7 30.7 %all_gather.27 = bf16[1024,128]{1,0:T(8,128)(2,1)S(1)} all-gather(bf16[128,128]{1,0:T(8,128)(2,1)S(1)} %copy-done.176), channel_id=1, replica_groups=mesh['dp'=8,'tensor'=4] {'dp'}, dimensions={0}, use_global_device_ids=true | all-gather | bytes 294912 | tf_op jit(solution)/shard_map/all_gather | solution.py:126
  603.7 16.5 collective-permute-done.12
  632.4 17.4 multiply_convert_fusion
  656.6 62.4 %reduce-scatter.14.cloned.1.call-done = f32[3264,128]{1,0:T(8,128)} async-done(((f32[3264,512]{1,0:T(8,128)}), f32[3264,128]{1,0:T(8,128)}) %reduce-scatter.14.cloned.1.call-update) | async-done | bytes 1671184 | tf_op jit(solution)/shard_map/reduce_scatter | solution.py:38
  740.4 12.0 all-reduce.126
  760.9 17.0 collective-permute-done.15
  804.3 63.8 %reduce-scatter.16.cloned.1.call-done = f32[3264,128]{1,0:T(8,128)} async-done(((f32[3264,512]{1,0:T(8,128)}), f32[3264,128]{1,0:T(8,128)}) %reduce-scatter.16.cloned.1.call-update) | async-done | bytes 1671184 | tf_op jit(solution)/shard_map/reduce_scatter | solution.py:38
  901.2 11.2 fusion.54
  922.3 105.5 %reduce-scatter.18.cloned.1.call-done = f32[6528,128]{1,0:T(8,128)} async-done(((f32[6528,512]{1,0:T(8,128)}), f32[6528,128]{1,0:T(8,128)}) %reduce-scatter.18.cloned.1.call-update) | async-done | bytes 3342352 | tf_op jit(solution)/shard_map/reduce_scatter | solution.py:38
  1062.2 25.9 %reduce-scatter.20.cloned.1.call-done = f32[476,128]{1,0:T(8,128)} async-done(((f32[476,512]{1,0:T(8,128)}), f32[476,128]{1,0:T(8,128)}) %reduce-scatter.20.cloned.1.call-update) | async-done | bytes 243728 | tf_op jit(solution)/shard_map/reduce_scatter | solution.py:38
  1097.4 13.3 fusion.59
  1110.6 17.5 reshape.245
  1147.2 17.1 fusion.61
  1164.3 30.2 %reshape.243 = f32[4,68,34816]{2,1,0:T(8,128)} reshape(f32[272,34816]{1,0:T(8,128)} %fusion.61) | data formatting | bytes 75759616 | tf_op jit(solution)/shard_map/reshape | solution.py:218
  1234.2 14.3 pad_add_fusion
  1256.1 22.5 reduce-scatter.22.cloned.1.call-done
  1342.0 12.8 fusion.58
  1354.9 15.0 fusion.60
  1370.7 22.1 all-reduce.121
  1395.0 39.1 %reduce-scatter.24.cloned.1.call-done = f32[3264,128]{1,0:T(8,128)} async-done(((f32[3264,512]{1,0:T(8,128)}), f32[3264,128]{1,0:T(8,128)}) %reduce-scatter.24.cloned.1.call-update) | async-done | bytes 1671184 | tf_op jit(solution)/shard_map/reduce_scatter | solution.py:38
  1442.7 97.6 %all-reduce.133.cloned.1.call-done = (f32[512,512]{1,0:T(8,128)}, f32[512,512]{1,0:T(8,128)}) async-done(((f32[512,512]{1,0:T(8,128)}, f32[512,512]{1,0:T(8,128)}), (f32[512,512]{1,0:T(8,128)}, f32[512,512]{1,0:T(8,128)})) %all-reduce.133.cloned.1.call-update) | async-done | bytes 2097168 | tf_op jit(solution)/shard_map/psum | solution.py:256
  1540.4 65.4 %reduce-scatter.38.cloned.1.call-done = f32[128,128]{1,0:T(8,128)} async-done(((f32[1024,128]{1,0:T(8,128)}), f32[128,128]{1,0:T(8,128)}) %reduce-scatter.38.cloned.1.call-update) | async-done | bytes 65552 | tf_op jit(solution)/shard_map/reduce_scatter | solution.py:243
  1605.8 78.3 %reduce-scatter.30.cloned.1.call-done = f32[64,12,128]{2,0,1:T(8,128)} async-done(((f32[512,12,128]{2,0,1:T(8,128)}), f32[64,12,128]{2,0,1:T(8,128)}) %reduce-scatter.30.cloned.1.call-update) | async-done | bytes 393232 | tf_op jit(solution)/shard_map/reduce_scatter | solution.py:239
  1684.1 78.3 %reduce-scatter.26.cloned.1.call-done = f32[768,128]{1,0:T(8,128)} async-done(((f32[6144,128]{1,0:T(8,128)}), f32[768,128]{1,0:T(8,128)}) %reduce-scatter.26.cloned.1.call-update) | async-done | bytes 393232 | tf_op jit(solution)/shard_map/reduce_scatter | solution.py:237
  1762.5 91.7 %reduce-scatter.32.cloned.1.call-done = f32[1024,128]{1,0:T(8,128)} async-done(((f32[8192,128]{1,0:T(8,128)}), f32[1024,128]{1,0:T(8,128)}) %reduce-scatter.32.cloned.1.call-update) | async-done | bytes 524304 | tf_op jit(solution)/shard_map/reduce_scatter | solution.py:240
  1854.2 222.1 %reduce-scatter.34.cloned.1.call-done = f32[3264,128]{1,0:T(8,128)} async-done(((f32[26112,128]{1,0:T(8,128)}), f32[3264,128]{1,0:T(8,128)}) %reduce-scatter.34.cloned.1.call-update) | async-done | bytes 1671184 | tf_op jit(solution)/shard_map/reduce_scatter | solution.py:241
  2076.3 302.3 %reduce-scatter.28.cloned.1.call-done = f32[4352,128]{1,0:T(8,128)} async-done(((f32[34816,128]{1,0:T(8,128)}), f32[4352,128]{1,0:T(8,128)}) %reduce-scatter.28.cloned.1.call-update) | async-done | bytes 2228240 | tf_op jit(solution)/shard_map/reduce_scatter | solution.py:238
  (851 shorter events, 751.8 us)
Async XLA Ops:
  7.2 49.9 %all-gather.7.cloned.1.call-start = ((), (), s32[]{:S(2)}) async-start(), calls=%async_computation.13 | async-start | bytes 1769472 | tf_op jit(solution)/shard_map/all_gather | solution.py:120
  7.9 99.5 %all-gather.9.cloned.1.call-start = ((), (), s32[]{:S(2)}) async-start(), calls=%async_computation.14 | async-start | bytes 2359296 | tf_op jit(solution)/shard_map/all_gather | solution.py:123
  8.7 433.3 %all-gather.13.cloned.1.call-start = ((), (), s32[]{:S(2)}) async-start(), calls=%async_computation.16 | async-start | bytes 7520256 | tf_op jit(solution)/shard_map/all_gather | solution.py:124
  9.4 441.9 %all-gather.11.cloned.1.call-start = ((), (), s32[]{:S(2)}) async-start(), calls=%async_computation.15 | async-start | bytes 10027008 | tf_op jit(solution)/shard_map/all_gather | solution.py:121
  10.0 463.5 %all-gather.15.cloned.1.call-start = ((), (), s32[]{:S(2)}) async-start(), calls=%async_computation.17 | async-start | bytes 1769472 | tf_op jit(solution)/shard_map/all_gather | solution.py:122
  10.0 19.1 collective-permute-start
  10.5 22.3 collective-permute-start.1
  12.6 472.1 %all-gather.17.cloned.1.call-start = ((), (), s32[]{:S(2)}) async-start(), calls=%async_computation.18 | async-start | bytes 2359296 | tf_op jit(solution)/shard_map/all_gather | solution.py:125
  29.2 11.9 collective-permute-start.2
  113.6 605.3 %reduce-scatter.14.cloned.1.call-start = ((), (), s32[]{:S(2)}) async-start(), calls=%async_computation.19 | async-start | bytes 8355840 | tf_op jit(solution)/shard_map/reduce_scatter | solution.py:38
  512.9 36.2 %collective-permute-start.9 = (bf16[6528,128]{1,0:T(8,128)(2,1)S(1)}, bf16[6528,128]{1,0:T(8,128)(2,1)S(1)}, u32[]{:S(2)}, u32[]{:S(2)}) collective-permute-start(bf16[6528,128]{1,0:T(8,128)(2,1)S(1)} %get-tuple-element.284), channel_id=1, source_target_pairs={{0,1},{1,2},{2,3},{3,0},{4,5},{5,6},{6,7},{7,4},{8,9},{9,10},{10,1... | collective-permute-start | bytes 5013512 | tf_op jit(solution)/shard_map/ppermute | solution.py:23
  513.7 69.1 %collective-permute-start.10 = (bf16[6528,128]{1,0:T(8,128)(2,1)S(1)}, bf16[6528,128]{1,0:T(8,128)(2,1)S(1)}, u32[]{:S(2)}, u32[]{:S(2)}) collective-permute-start(bf16[6528,128]{1,0:T(8,128)(2,1)S(1)} %get-tuple-element.284), channel_id=1, source_target_pairs={{0,3},{1,0},{2,1},{3,2},{4,7},{5,4},{6,5},{7,6},{8,11},{9,8},{10,9... | collective-permute-start | bytes 5013512 | tf_op jit(solution)/shard_map/ppermute | solution.py:26
  549.2 34.1 %collective-permute-start.11 = (bf16[6528,128]{1,0:T(8,128)(2,1)S(1)}, bf16[6528,128]{1,0:T(8,128)(2,1)S(1)}, u32[]{:S(2)}, u32[]{:S(2)}) collective-permute-start(bf16[6528,128]{1,0:T(8,128)(2,1)S(1)} %collective-permute-done.9), channel_id=1, source_target_pairs={{0,1},{1,2},{2,3},{3,0},{4,5},{5,6},{6,7},{7,4},{8,9},{9,10},{10,1... | collective-permute-start | bytes 5013512 | tf_op jit(solution)/shard_map/ppermute | solution.py:23
  601.9 18.3 collective-permute-start.12
  602.7 20.3 collective-permute-start.13
  620.3 11.9 collective-permute-start.14
  656.3 211.8 %reduce-scatter.16.cloned.1.call-start = ((), (), s32[]{:S(2)}) async-start(), calls=%async_computation.20 | async-start | bytes 8355840 | tf_op jit(solution)/shard_map/reduce_scatter | solution.py:38
  759.1 18.8 collective-permute-start.15
  759.3 20.0 collective-permute-start.16
  777.9 11.9 collective-permute-start.17
  804.3 223.5 %reduce-scatter.18.cloned.1.call-start = ((), (), s32[]{:S(2)}) async-start(), calls=%async_computation.21 | async-start | bytes 16711680 | tf_op jit(solution)/shard_map/reduce_scatter | solution.py:38
  922.2 165.8 %reduce-scatter.20.cloned.1.call-start = ((), (), s32[]{:S(2)}) async-start(), calls=%async_computation.22 | async-start | bytes 1228800 | tf_op jit(solution)/shard_map/reduce_scatter | solution.py:38
  1062.2 216.3 %reduce-scatter.22.cloned.1.call-start = ((), (), s32[]{:S(2)}) async-start(), calls=%async_computation.23 | async-start | bytes 1228800 | tf_op jit(solution)/shard_map/reduce_scatter | solution.py:38
  1252.7 140.1 %reduce-scatter.36.cloned.1.call-start = ((), (), s32[]{:S(2)}) async-start(), calls=%async_computation.30 | async-start | bytes 4718592 | tf_op jit(solution)/shard_map/reduce_scatter | solution.py:242
  1255.8 178.3 %reduce-scatter.24.cloned.1.call-start = ((), (), s32[]{:S(2)}) async-start(), calls=%async_computation.24 | async-start | bytes 8355840 | tf_op jit(solution)/shard_map/reduce_scatter | solution.py:38
  1313.2 227.1 %all-reduce.133.cloned.1.call-start = ((), (), s32[]{:S(2)}) async-start(), calls=%async_computation.32 | async-start | bytes 4194304 | tf_op jit(solution)/shard_map/psum | solution.py:256
  1322.3 283.5 %reduce-scatter.38.cloned.1.call-start = ((), (), s32[]{:S(2)}) async-start(), calls=%async_computation.31 | async-start | bytes 589824 | tf_op jit(solution)/shard_map/reduce_scatter | solution.py:243
  1328.3 355.8 %reduce-scatter.30.cloned.1.call-start = ((), (), s32[]{:S(2)}) async-start(), calls=%async_computation.27 | async-start | bytes 3538944 | tf_op jit(solution)/shard_map/reduce_scatter | solution.py:239
  1331.1 431.3 %reduce-scatter.26.cloned.1.call-start = ((), (), s32[]{:S(2)}) async-start(), calls=%async_computation.25 | async-start | bytes 3538944 | tf_op jit(solution)/shard_map/reduce_scatter | solution.py:237
  1336.3 517.8 %reduce-scatter.32.cloned.1.call-start = ((), (), s32[]{:S(2)}) async-start(), calls=%async_computation.28 | async-start | bytes 4718592 | tf_op jit(solution)/shard_map/reduce_scatter | solution.py:240
  1342.0 734.3 %reduce-scatter.34.cloned.1.call-start = ((), (), s32[]{:S(2)}) async-start(), calls=%async_computation.29 | async-start | bytes 15040512 | tf_op jit(solution)/shard_map/reduce_scatter | solution.py:241
  1354.8 1023.8 %reduce-scatter.28.cloned.1.call-start = ((), (), s32[]{:S(2)}) async-start(), calls=%async_computation.26 | async-start | bytes 20054016 | tf_op jit(solution)/shard_map/reduce_scatter | solution.py:238
  (202 other events, 8728.2 us)
Sparse Core Ops, SparseCore 0:
  10.2 46.8 all-gather.6
  59.3 48.0 all-gather.8
  109.6 102.3 all-gather.12
  214.1 129.7 all-gather.10
  345.9 42.3 all-gather.14
  390.3 48.0 all-gather.16
  656.4 62.4 reduce-scatter.13
  804.4 63.7 reduce-scatter.15
  922.4 105.4 reduce-scatter.17
  1062.3 25.7 reduce-scatter.19
  1252.8 25.6 reduce-scatter.21
  1282.0 88.4 reduce-scatter.35
  1373.2 60.8 reduce-scatter.23
  1438.2 102.0 all-reduce.132
  1544.1 61.6 reduce-scatter.37
  1610.3 73.8 reduce-scatter.29
  1688.6 73.8 reduce-scatter.25
  1767.0 87.1 reduce-scatter.31
  1858.4 217.8 reduce-scatter.33
  2081.2 297.3 reduce-scatter.27
